TPU v7x, 512 devices: a whole 4x4x16 slice. The times are simulated.
512 devices in a mesh: sector: 16 (over y, x_lo, core), dom: 32 (over z, x_hi).
Axes of the slice: x: 4 (x_hi: 2, x_lo: 2; x = x_hi * 2 + x_lo), y: 4, z: 16, core: 2. Of those that a mesh axis runs over, the one named last changes fastest.
Arguments:
- amplitudes: float32 [64, 48], replicated, may hold values from -0.3 to 0.3
- mode_shapes: float32 [48, 3, 524288], P(None, None, ('sector', 'dom')), may hold values from -6 to 6
- shape_grads: float32 [8, 3, 524288], P(None, None, ('sector', 'dom')), may hold values from -2.4 to 2.4
- lame_params: float32 [2, 524288], P(None, ('sector', 'dom')), may hold values from 0.5 to 2
- connectivity: int32 [8, 524288], P(None, ('sector', 'dom')), may hold values from -1 to 1791, as said below
- dom_sends: int32 [2, 131072], P(None, ('sector', 'dom')), may hold values from -1 to 1023, as said below
- sector_sends: int32 [2, 65536], P(None, ('sector', 'dom')), may hold values from -1 to 1023, as said below
Outputs:
- nodal_force: float32 [64, 3, 524288], P(None, None, ('sector', 'dom'))
- modal_force: float32 [64, 48], replicated
Inputs may be any that keep to these rules, and one draw needn't show every extreme that they name: `connectivity`: in each device's block, the live elements come first and the padding element slots after them hold -1 in all 8 rows; a live slot names a slot of the device's extended table. Some device has all 1024 slots live. `dom_sends`: each device's row lists its own node numbers first, then -1; a row holds 128 to 256 live entries, and some row is full. `sector_sends`: each device's row lists its own node numbers first, then -1; a row holds 64 to 128 live entries, and some row is full.
All inputs are finite; a program needn't handle non-finite values.
Results may differ from a plain program's by a relative error of at most 0.0003.
Values sent between devices are 32-bit elements; how exact they have to be, the bound alone decides.
A program may use at most 64 MiB of HBM per device.

v0:
```python
import math

import jax
import jax.numpy as jnp
from jax import lax
from jax.sharding import PartitionSpec as P


def padded(cells, sides, width, closed):
    for axis, dim in sides:
        count = lax.axis_size(axis)
        ends = count if closed else count - 1
        head = lax.slice_in_dim(cells, 0, width, axis=dim)
        tail = lax.slice_in_dim(cells, cells.shape[dim] - width, cells.shape[dim], axis=dim)
        cells = jnp.concatenate(
            [
                lax.ppermute(tail, axis, [(i, (i + 1) % count) for i in range(ends)]),
                cells,
                lax.ppermute(head, axis, [((i + 1) % count, i) for i in range(ends)]),
            ],
            axis=dim,
        )
    return cells


def take_slots(node_table, send_lists):
    slot_width = node_table.shape[1]
    slot_index = jnp.where(send_lists < 0, slot_width, send_lists).reshape(-1)
    return jnp.take(node_table, slot_index, axis=1, mode="fill", fill_value=0.0)


def add_slots(node_table, send_lists, add_values):
    slot_width = node_table.shape[1]
    slot_index = jnp.where(send_lists < 0, slot_width, send_lists).reshape(-1)
    return node_table.at[:, slot_index].add(add_values, mode="drop")


def element_forces(accum, extended, connect, gradients, lame):
    ext_width = extended.shape[1]
    combo_total = extended.shape[0] // 3
    elem_total = connect.shape[1]
    slot_index = jnp.where(connect < 0, ext_width, connect).reshape(-1)
    corners = jnp.take(extended, slot_index, axis=1, mode="fill", fill_value=0.0).reshape(
        combo_total, 3, 8, elem_total
    )
    gradient = jnp.zeros((combo_total, 3, 3, elem_total), extended.dtype)
    for corner in range(8):
        gradient = gradient + corners[:, :, None, corner, :] * gradients[corner][None, None, :, :]
    quadratic = jnp.sum(gradient[:, :, :, None, :] * gradient[:, :, None, :, :], axis=1)
    green_strain = 0.5 * (gradient + jnp.swapaxes(gradient, 1, 2) + quadratic)
    strain_trace = green_strain[:, 0, 0] + green_strain[:, 1, 1] + green_strain[:, 2, 2]
    identity = jnp.eye(3, dtype=extended.dtype)[None, :, :, None]
    stress = lame[0] * strain_trace[:, None, None, :] * identity + 2.0 * lame[1] * green_strain
    piola = stress + jnp.sum(gradient[:, :, :, None, :] * stress[:, None, :, :, :], axis=2)
    corner_forces = jnp.stack(
        [jnp.sum(piola * gradients[corner][None, None, :, :], axis=2) for corner in range(8)],
        axis=2,
    )
    return accum.at[:, slot_index].add(
        corner_forces.reshape(3 * combo_total, 8 * elem_total), mode="drop"
    )


def outer_ends(ext_rows, slot_width):
    return jnp.concatenate([ext_rows[:, :slot_width], ext_rows[:, 3 * slot_width :]], axis=1)


def local(amplitudes, mode_shapes, shape_grads, lame_params, connectivity, dom_sends, sector_sends):
    modes_total, _, node_total = mode_shapes.shape
    combo_total = amplitudes.shape[0]
    table_rows = 3 * combo_total
    dom_width = dom_sends.shape[1]
    sec_width = sector_sends.shape[1]
    flat_shapes = mode_shapes.reshape(modes_total, 3 * node_total)
    displaced = jnp.dot(
        amplitudes, flat_shapes, precision=lax.Precision.HIGHEST, preferred_element_type=jnp.float32
    ).reshape(table_rows, node_total)
    dom_ext = padded(take_slots(displaced, dom_sends), (("dom", 1),), dom_width, False)
    sec_ext = padded(take_slots(displaced, sector_sends), (("sector", 1),), sec_width, True)
    halo_moved = jnp.concatenate(
        [outer_ends(dom_ext, dom_width), outer_ends(sec_ext, sec_width)], axis=1
    )
    extended = jnp.concatenate([displaced, halo_moved], axis=1)
    ext_width = extended.shape[1]
    elem_total = connectivity.shape[1]
    block_size = math.gcd(elem_total, 256)
    turn_total = elem_total // block_size

    def one_block(turn_index, forces):
        first_col = turn_index * block_size
        connect_block = lax.dynamic_slice_in_dim(connectivity, first_col, block_size, 1)
        grads_block = lax.dynamic_slice_in_dim(shape_grads, first_col, block_size, 2)
        lame_block = lax.dynamic_slice_in_dim(lame_params, first_col, block_size, 1)
        return element_forces(forces, extended, connect_block, grads_block, lame_block)

    slot_forces = lax.fori_loop(
        0, turn_total, one_block, jnp.zeros((table_rows, ext_width), jnp.float32)
    )
    own_forces = slot_forces[:, :node_total]
    dom_back = slot_forces[:, node_total : node_total + 2 * dom_width]
    sec_back = slot_forces[:, node_total + 2 * dom_width :]
    dom_return = padded(dom_back, (("dom", 1),), dom_width, False)
    own_forces = add_slots(own_forces, dom_sends, outer_ends(dom_return, dom_width))
    sec_return = padded(sec_back, (("sector", 1),), sec_width, True)
    own_forces = add_slots(own_forces, sector_sends, outer_ends(sec_return, sec_width))
    partial_modal = lax.dot_general(
        own_forces.reshape(combo_total, 3 * node_total),
        flat_shapes,
        (((1,), (1,)), ((), ())),
        precision=lax.Precision.HIGHEST,
        preferred_element_type=jnp.float32,
    )
    modal_total = lax.psum(partial_modal, ("sector", "dom"))
    all_nodes = node_total * lax.axis_size("sector") * lax.axis_size("dom")
    return (
        own_forces.reshape(combo_total, 3, node_total),
        modal_total / math.sqrt(3.0 * all_nodes),
    )


def solution(mesh):
    placed = (
        P(),
        P(None, None, ("sector", "dom")),
        P(None, None, ("sector", "dom")),
        P(None, ("sector", "dom")),
        P(None, ("sector", "dom")),
        P(None, ("sector", "dom")),
        P(None, ("sector", "dom")),
    )
    return jax.shard_map(
        local,
        mesh=mesh,
        in_specs=placed,
        out_specs=(P(None, None, ("sector", "dom")), P()),
        check_vma=False,
    )
```

profile of v0, /device:TPU:1, one launch (start us, length us, event | category | flops | bytes accessed | tf_op | source)
XLA Modules:
  0.0 308.0 jit_solution(2652404135059010113)
XLA Ops:
  0.6 0.7 compare_select_fusion.8
  1.3 0.7 fusion.11
  2.1 1.1 copy.105
  3.2 0.8 copy-done.2
  4.0 0.8 fusion.17
  5.3 1.6 gather_fusion.1
  7.1 5.5 %collective-permute-start = (f32[192,256]{0,1:T(8,128)S(1)}, f32[192,256]{0,1:T(8,128)S(1)}, u32[]{:S(2)}, u32[]{:S(2)}) collective-permute-start(f32[192,256]{0,1:T(8,128)S(1)} %get-tuple-element.244), channel_id=1, source_target_pairs={{0,1},{1,2},{2,3},{3,4},{4,5},{5,6},{6,7},{7,8},{8,9},{9,10},{10,1... | collective-permute-start | bytes 589832 | tf_op jit(solution)/shard_map/ppermute | solution.py:17
  12.6 1.0 gather_fusion.2
  13.7 4.6 %collective-permute-start.3 = (f32[192,128]{0,1:T(8,128)S(1)}, f32[192,128]{0,1:T(8,128)S(1)}, u32[]{:S(2)}, u32[]{:S(2)}) collective-permute-start(f32[192,128]{0,1:T(8,128)S(1)} %get-tuple-element.245), channel_id=1, source_target_pairs={{32,0},{64,32},{96,64},{128,96},{160,128},{192,160},{224,192},{256... | collective-permute-start | bytes 294920 | tf_op jit(solution)/shard_map/ppermute | solution.py:19
  18.4 1.9 collective-permute-start.2
  20.3 1.5 collective-permute-start.1
  21.9 9.2 %collective-permute-done.1 = f32[192,256]{0,1:T(8,128)S(1)} collective-permute-done((f32[192,256]{0,1:T(8,128)S(1)}, f32[192,256]{0,1:T(8,128)S(1)}, u32[]{:S(2)}, u32[]{:S(2)}) %collective-permute-start.1) | collective-permute-done | bytes 196640 | tf_op jit(solution)/shard_map/ppermute | solution.py:19
  31.3 1.1 copy-done.1
  32.4 136.4 %while.15 = (s32[]{:T(128)}, f32[192,1792]{0,1:T(8,128)S(1)}, s32[8,1024]{1,0:T(8,128)S(1)}, f32[2,1024]{1,0:T(2,128)}, f32[192,1792]{0,1:T(8,128)}, /*index=5*/...) while((s32[]{:T(128)}, f32[192,1792]{0,1:T(8,128)S(1)}, ...), condition=%wide.region_12.13_spmd, body=%wide.region_0.12_spmd.sunk | while | flops 12415007 | bytes 49229240 | solution.py:96
  32.4 0.8 constant_dynamic-slice_fusion.12
  33.3 1.3 constant_dynamic-slice_fusion.11
  34.6 10.1 %gather_fusion = f32[2048,192]{1,0:T(8,128)} fusion(f32[192,1792]{0,1:T(8,128)} %get-tuple-element.414, s32[2048]{0:T(1024)S(1)} %broadcast_clamp_fusion.2), kind=kCustom, calls=%fused_computation.clone.1 | custom fusion | bytes 3153920 | tf_op jit(solution)/shard_map/while/body/eval_jaxpr/jit(_take)/gather | solution.py:43
  44.7 1.9 copy.147
  46.6 0.6 copy.148
  47.3 1.1 fusion.28
  50.4 0.9 copy.149
  51.3 0.6 copy.150
  51.9 1.8 copy.151
  53.8 12.6 %scatter_fusion = f32[192,1792]{0,1:T(8,128)S(1)} fusion(f32[192,1792]{0,1:T(8,128)S(1)} %get-tuple-element.394, s32[2048]{0:T(1024)S(1)} %bitcast.158, f32[2048,192]{1,0:T(8,128)} %copy.151), kind=kCustom, calls=%fused_computation.3.clone.1 | custom fusion | flops 393216 | bytes 4726784 | tf_op jit(solution)/shard_map/while/body/eval_jaxpr/scatter-add | solution.py:59
  66.5 0.8 constant_dynamic-slice_fusion.12
  67.4 1.4 constant_dynamic-slice_fusion.11
  68.8 10.1 %gather_fusion = f32[2048,192]{1,0:T(8,128)} fusion(f32[192,1792]{0,1:T(8,128)} %get-tuple-element.414, s32[2048]{0:T(1024)S(1)} %broadcast_clamp_fusion.2), kind=kCustom, calls=%fused_computation.clone.1 | custom fusion | bytes 3153920 | tf_op jit(solution)/shard_map/while/body/eval_jaxpr/jit(_take)/gather | solution.py:43
  78.8 1.9 copy.147
  81.4 1.1 fusion.28
  84.5 0.9 copy.149
  86.0 1.8 copy.151
  87.9 12.6 %scatter_fusion = f32[192,1792]{0,1:T(8,128)S(1)} fusion(f32[192,1792]{0,1:T(8,128)S(1)} %get-tuple-element.394, s32[2048]{0:T(1024)S(1)} %bitcast.158, f32[2048,192]{1,0:T(8,128)} %copy.151), kind=kCustom, calls=%fused_computation.3.clone.1 | custom fusion | flops 393216 | bytes 4726784 | tf_op jit(solution)/shard_map/while/body/eval_jaxpr/scatter-add | solution.py:59
  100.6 0.8 constant_dynamic-slice_fusion.12
  101.5 1.3 constant_dynamic-slice_fusion.11
  102.8 10.1 %gather_fusion = f32[2048,192]{1,0:T(8,128)} fusion(f32[192,1792]{0,1:T(8,128)} %get-tuple-element.414, s32[2048]{0:T(1024)S(1)} %broadcast_clamp_fusion.2), kind=kCustom, calls=%fused_computation.clone.1 | custom fusion | bytes 3153920 | tf_op jit(solution)/shard_map/while/body/eval_jaxpr/jit(_take)/gather | solution.py:43
  112.9 1.9 copy.147
  115.5 1.1 fusion.28
  118.6 0.9 copy.149
  119.5 0.6 copy.150
  120.1 1.8 copy.151
  122.0 12.6 %scatter_fusion = f32[192,1792]{0,1:T(8,128)S(1)} fusion(f32[192,1792]{0,1:T(8,128)S(1)} %get-tuple-element.394, s32[2048]{0:T(1024)S(1)} %bitcast.158, f32[2048,192]{1,0:T(8,128)} %copy.151), kind=kCustom, calls=%fused_computation.3.clone.1 | custom fusion | flops 393216 | bytes 4726784 | tf_op jit(solution)/shard_map/while/body/eval_jaxpr/scatter-add | solution.py:59
  134.7 0.8 constant_dynamic-slice_fusion.12
  135.6 1.4 constant_dynamic-slice_fusion.11
  137.0 10.1 %gather_fusion = f32[2048,192]{1,0:T(8,128)} fusion(f32[192,1792]{0,1:T(8,128)} %get-tuple-element.414, s32[2048]{0:T(1024)S(1)} %broadcast_clamp_fusion.2), kind=kCustom, calls=%fused_computation.clone.1 | custom fusion | bytes 3153920 | tf_op jit(solution)/shard_map/while/body/eval_jaxpr/jit(_take)/gather | solution.py:43
  147.0 1.9 copy.147
  148.9 0.6 copy.148
  149.6 1.1 fusion.28
  152.7 0.9 copy.149
  153.6 0.6 copy.150
  154.2 1.8 copy.151
  156.1 12.6 %scatter_fusion = f32[192,1792]{0,1:T(8,128)S(1)} fusion(f32[192,1792]{0,1:T(8,128)S(1)} %get-tuple-element.394, s32[2048]{0:T(1024)S(1)} %bitcast.158, f32[2048,192]{1,0:T(8,128)} %copy.151), kind=kCustom, calls=%fused_computation.3.clone.1 | custom fusion | flops 393216 | bytes 4726784 | tf_op jit(solution)/shard_map/while/body/eval_jaxpr/scatter-add | solution.py:59
  168.8 2.8 collective-permute-start.4
  171.6 1.3 collective-permute-start.5
  172.9 0.7 fusion.13
  173.6 4.8 %collective-permute-start.6 = (f32[192,128]{0,1:T(8,128)}, f32[192,128]{0,1:T(8,128)}, u32[]{:S(2)}, u32[]{:S(2)}) collective-permute-start(f32[192,128]{0,1:T(8,128)} %get-tuple-element.239), channel_id=1, source_target_pairs={{0,32},{32,64},{64,96},{96,128},{128,160},{160,192},{192,224},{224... | collective-permute-start | bytes 294920 | tf_op jit(solution)/shard_map/ppermute | solution.py:17
  178.4 2.2 collective-permute-start.7
  180.7 3.8 %scatter_custom_fusion.1 = f32[192,1024]{0,1:T(8,128)S(1)} fusion(f32[192,1024]{0,1:T(8,128)S(1)} %slice.257, s32[512]{0:T(512)S(1)} %bitcast.167, f32[192,256]{0,1:T(8,128)S(1)} %collective-permute-done.5, f32[]{:T(128)} %constant.154, f32[192,256]{0,1:T(8,128)S(1)} %collective-permute-done.4), kind=kCustom, calls=%fused_computation.67 | custom fusion | flops 196608 | bytes 1310724 | tf_op jit(solution)/shard_map/scatter-add | solution.py:35
  184.5 0.9 collective-permute-done.6
  185.4 4.3 %collective-permute-done.7 = f32[192,128]{0,1:T(8,128)} collective-permute-done((f32[192,128]{0,1:T(8,128)}, f32[192,128]{0,1:T(8,128)}, u32[]{:S(2)}, u32[]{:S(2)}) %collective-permute-start.7) | collective-permute-done | bytes 98336 | tf_op jit(solution)/shard_map/ppermute | solution.py:19
  189.6 3.0 scatter_custom_fusion.2
  194.1 0.8 fusion.18
  194.8 111.2 %psum.7 = f32[64,48]{0,1:T(8,128)S(1)} all-reduce(f32[64,48]{0,1:T(8,128)S(1)} %fusion.18), channel_id=1, replica_groups=mesh['sector'=16,'dom'=32] {'sector','dom'}, use_global_device_ids=true, to_apply=%region_15.16 | all-reduce | flops 3072 | bytes 24576 | tf_op jit(solution)/shard_map/psum | solution.py:113
  306.0 0.6 broadcast_multiply_fusion.1
  306.6 1.3 copy.92
  (162 shorter events, 12.6 us)
Async XLA Ops:
  0.6 3.4 %copy-start = (f32[64,48]{0,1:T(8,128)S(1)}, f32[64,48]{0,1:T(8,128)}, u32[]{:S(2)}) copy-start(f32[64,48]{0,1:T(8,128)} %param.9) | copy-start | bytes 36868
  3.2 0.8 copy-start.2
  6.9 5.7 %copy-start.5 = (s32[2,128]{1,0:T(2,128)S(1)}, s32[2,128]{1,0:T(2,128)}, u32[]{:S(2)}) copy-start(s32[2,128]{1,0:T(2,128)} %param.15) | copy-start | bytes 3076
  7.1 14.8 %collective-permute-start = (f32[192,256]{0,1:T(8,128)S(1)}, f32[192,256]{0,1:T(8,128)S(1)}, u32[]{:S(2)}, u32[]{:S(2)}) collective-permute-start(f32[192,256]{0,1:T(8,128)S(1)} %get-tuple-element.244), channel_id=1, source_target_pairs={{0,1},{1,2},{2,3},{3,4},{4,5},{5,6},{6,7},{7,8},{8,9},{9,10},{10,1... | collective-permute-start | bytes 589832 | tf_op jit(solution)/shard_map/ppermute | solution.py:17
  13.7 17.4 %collective-permute-start.3 = (f32[192,128]{0,1:T(8,128)S(1)}, f32[192,128]{0,1:T(8,128)S(1)}, u32[]{:S(2)}, u32[]{:S(2)}) collective-permute-start(f32[192,128]{0,1:T(8,128)S(1)} %get-tuple-element.245), channel_id=1, source_target_pairs={{32,0},{64,32},{96,64},{128,96},{160,128},{192,160},{224,192},{256... | collective-permute-start | bytes 294920 | tf_op jit(solution)/shard_map/ppermute | solution.py:19
  18.4 12.7 %collective-permute-start.2 = (f32[192,128]{0,1:T(8,128)S(1)}, f32[192,128]{0,1:T(8,128)S(1)}, u32[]{:S(2)}, u32[]{:S(2)}) collective-permute-start(f32[192,128]{0,1:T(8,128)S(1)} %get-tuple-element.246), channel_id=1, source_target_pairs={{0,32},{32,64},{64,96},{96,128},{128,160},{160,192},{192,224},{224... | collective-permute-start | bytes 294920 | tf_op jit(solution)/shard_map/ppermute | solution.py:17
  20.3 10.8 %collective-permute-start.1 = (f32[192,256]{0,1:T(8,128)S(1)}, f32[192,256]{0,1:T(8,128)S(1)}, u32[]{:S(2)}, u32[]{:S(2)}) collective-permute-start(f32[192,256]{0,1:T(8,128)S(1)} %get-tuple-element.243), channel_id=1, source_target_pairs={{1,0},{2,1},{3,2},{4,3},{5,4},{6,5},{7,6},{8,7},{9,8},{10,9},{11,1... | collective-permute-start | bytes 589832 | tf_op jit(solution)/shard_map/ppermute | solution.py:19
  21.9 10.5 %copy-start.4 = (s32[8,1024]{1,0:T(8,128)S(1)}, s32[8,1024]{1,0:T(8,128)}, u32[]{:S(2)}) copy-start(s32[8,1024]{1,0:T(8,128)} %param.13) | copy-start | bytes 98308
  31.1 1.2 copy-start.1
  168.8 11.9 %collective-permute-start.4 = (f32[192,256]{0,1:T(8,128)S(1)}, f32[192,256]{0,1:T(8,128)S(1)}, u32[]{:S(2)}, u32[]{:S(2)}) collective-permute-start(f32[192,256]{0,1:T(8,128)S(1)} %get-tuple-element.241), channel_id=1, source_target_pairs={{0,1},{1,2},{2,3},{3,4},{4,5},{5,6},{6,7},{7,8},{8,9},{9,10},{10,1... | collective-permute-start | bytes 589832 | tf_op jit(solution)/shard_map/ppermute | solution.py:17
  171.6 9.1 %collective-permute-start.5 = (f32[192,256]{0,1:T(8,128)S(1)}, f32[192,256]{0,1:T(8,128)S(1)}, u32[]{:S(2)}, u32[]{:S(2)}) collective-permute-start(f32[192,256]{0,1:T(8,128)S(1)} %get-tuple-element.242), channel_id=1, source_target_pairs={{1,0},{2,1},{3,2},{4,3},{5,4},{6,5},{7,6},{8,7},{9,8},{10,9},{11,1... | collective-permute-start | bytes 589832 | tf_op jit(solution)/shard_map/ppermute | solution.py:19
  173.6 11.8 %collective-permute-start.6 = (f32[192,128]{0,1:T(8,128)}, f32[192,128]{0,1:T(8,128)}, u32[]{:S(2)}, u32[]{:S(2)}) collective-permute-start(f32[192,128]{0,1:T(8,128)} %get-tuple-element.239), channel_id=1, source_target_pairs={{0,32},{32,64},{64,96},{96,128},{128,160},{160,192},{192,224},{224... | collective-permute-start | bytes 294920 | tf_op jit(solution)/shard_map/ppermute | solution.py:17
  178.4 11.3 %collective-permute-start.7 = (f32[192,128]{0,1:T(8,128)}, f32[192,128]{0,1:T(8,128)}, u32[]{:S(2)}, u32[]{:S(2)}) collective-permute-start(f32[192,128]{0,1:T(8,128)} %get-tuple-element.240), channel_id=1, source_target_pairs={{32,0},{64,32},{96,64},{128,96},{160,128},{192,160},{224,192},{256... | collective-permute-start | bytes 294920 | tf_op jit(solution)/shard_map/ppermute | solution.py:19
  193.0 1.1 copy-start.3
where the time goes:
time: 309 us; the launch traced here: 308 us
  blocking collectives  111 us (36%)
  local copies, waits for them, and re-layouts  87.5 us (28%)
  other arithmetic  66.7 us (22%)
  starting transfers between devices  24.6 us (8%)
  waiting for transfers between devices  14.3 us (5%)
    psum x1, blocking collectives, local(): modal_total = lax.psum(partial_modal, ('sector', 'dom'))  111 us
    scatter-add x4, other arithmetic, element_forces(): accum.at[:, slot_index]  50.6 us
    gather x8, local copies, waits for them, and re-layouts, element_forces(): jnp.take(extended, slot_index, axis=1, mode='fill', fill_value=0.0)  47.8 us
    ppermute x4, starting transfers between devices, padded(): lax.ppermute(tail, axis, [(i, (i + 1) % count) for i in range(ends)])  15 us
    ppermute x4, waiting for transfers between devices, padded(): lax.ppermute(head, axis, [((i + 1) % count, i) for i in range(ends)])  13.4 us
    ppermute x4, starting transfers between devices, padded(): lax.ppermute(head, axis, [((i + 1) % count, i) for i in range(ends)])  9.62 us
    reshape x4, local copies, waits for them, and re-layouts, element_forces(): corner_forces.reshape(3 * combo_total, 8 * elem_total)  7.39 us
    scatter-add x2, other arithmetic, add_slots(): return node_table.at[:, slot_index].add(add_values, mode='drop')  6.78 us
  transfers between devices with their start and end apart: 8, of which 3 were waited for; matrix products, arithmetic and copies ran while one was open for 2% of the time, Pallas kernels for 0%

commit v1 on v0

v1 whole, which is shorter than its diff:
```python
import functools
import math

import jax
import jax.numpy as jnp
from jax import lax
from jax.experimental import pallas as pl
from jax.experimental.pallas import tpu as pltpu
from jax.sharding import PartitionSpec as P

MESH = pl.DeviceIdType.MESH
F8 = jnp.float8_e4m3fn
BF = jnp.bfloat16
F32 = jnp.float32
TILE = 128
NT = (((1,), (1,)), ((), ()))


def bf_pieces(x):
    hi = x.astype(BF)
    return hi, (x - hi.astype(F32)).astype(BF)


def f8_pieces(x):
    a = x.astype(F8)
    rest = (x - a.astype(F32)) * 16.0
    b = rest.astype(F8)
    rest = (rest - b.astype(F32)) * 16.0
    return a, b, rest.astype(F8)


def joined(r, rows, unit):
    return r[:rows] * unit + (r[rows : 2 * rows] + r[2 * rows :] * 0.0625) * (unit * 0.0625)


def tile_hits(row, first, dtype_one, dtype_zero):
    near = row - first
    near = jnp.where((near >= 0) & (near < TILE), near, -1).astype(jnp.int8)
    slots = lax.broadcasted_iota(jnp.int32, (TILE, row.shape[1]), 0).astype(jnp.int8)
    return jnp.where(slots == near, dtype_one, dtype_zero)


def peak(x):
    return jnp.max(jnp.max(jnp.abs(x), axis=0, keepdims=True), axis=1, keepdims=True)


def stage_index(stage, y, x, c, z):
    return (x * 2 + c, y * 2 + z % 2, z // 2)[stage]


def stage_device(stage, i, y, x, c, z):
    if stage == 0:
        x, c = i // 2, i % 2
    elif stage == 1:
        y, z = i // 2, (z // 2) * 2 + i % 2
    else:
        z = i * 2 + z % 2
    return (y * 4 + (x % 2) * 2 + c, z * 2 + x // 2)


def kernel(
    scale, amp_ref, modes_ref, grads_ref, lame_ref, conn_ref, dsend_ref, ssend_ref,
    out_ref, modal_ref,
    hot, hot_send, hot_block, own_lhs, halo_lhs, corners, gmode, piola, forces,
    pk_dom, pk_sec, halo_dom, halo_sec, bk_dom, bk_sec, ret_dom, ret_sec, mine, theirs,
    fs_sem, fr_sem, bs_sem, br_sem, as_sem, ar_sem,
):
    n_sec, n_dom = lax.axis_size("sector"), lax.axis_size("dom")
    sec, dom = lax.axis_index("sector"), lax.axis_index("dom")
    modes, combos = amp_ref.shape
    nodes = modes_ref.shape[1]
    elems = conn_ref.shape[1]
    wd, ws = dsend_ref.shape[1], ssend_ref.shape[1]
    rows = 3 * modes
    frows = 3 * combos
    halo = 2 * wd + 2 * ws
    y, x, c, z = sec // 4, (dom % 2) * 2 + (sec // 2) % 2, sec % 2, dom // 2
    dom_lo, dom_hi = (sec, lax.rem(dom + n_dom - 1, n_dom)), (sec, lax.rem(dom + 1, n_dom))
    sec_lo, sec_hi = (lax.rem(sec + n_sec - 1, n_sec), dom), (lax.rem(sec + 1, n_sec), dom)
    halo_to = [dom_lo, dom_hi, sec_lo, sec_hi]
    me = [stage_index(s, y, x, c, z) for s in range(3)]
    groups = [
        [stage_device(s, lax.rem(me[s] + r, 8), y, x, c, z) for r in range(1, 8)] for s in range(3)
    ]

    barrier = pltpu.get_barrier_semaphore()
    everyone = halo_to + groups[0] + groups[1] + groups[2]
    for other in everyone:
        pl.semaphore_signal(barrier, inc=1, device_id=other, device_id_type=MESH)

    for first, width, send in ((0, wd, dsend_ref), (2 * wd, ws, ssend_ref)):
        for row in range(2):
            cols = pl.ds(first + row * width, width)
            slots = lax.broadcasted_iota(jnp.int32, (nodes, width), 0)
            hot_send[:, cols] = jnp.where(slots == send[row : row + 1, :], 1.0, 0.0).astype(BF)

    shapes = modes_ref[...]
    packets = jnp.dot(
        jnp.concatenate(bf_pieces(shapes), axis=0), hot_send[...], preferred_element_type=F32
    )
    packets = packets[:rows] + packets[rows:]
    for row in range(2):
        pk_dom[row] = packets[:, row * wd : (row + 1) * wd]
        pk_sec[row] = packets[:, 2 * wd + row * ws : 2 * wd + (row + 1) * ws]

    pl.semaphore_wait(barrier, len(everyone))
    forward = []
    for j, (src, dst) in enumerate(
        (
            (pk_dom.at[0], halo_dom.at[1]),
            (pk_dom.at[1], halo_dom.at[0]),
            (pk_sec.at[0], halo_sec.at[1]),
            (pk_sec.at[1], halo_sec.at[0]),
        )
    ):
        forward.append(
            pltpu.make_async_remote_copy(
                src_ref=src, dst_ref=dst, send_sem=fs_sem.at[j], recv_sem=fr_sem.at[j],
                device_id=halo_to[j], device_id_type=MESH,
            )
        )
        forward[-1].start()

    one8, zero8 = jnp.ones((TILE, elems), F8), jnp.zeros((TILE, elems), F8)

    def build(a, carry):
        row = conn_ref[pl.ds(a, 1), :]
        cols = pl.ds(pl.multiple_of(a * elems, elems), elems)
        for t in range((nodes + halo) // TILE):
            hot[pl.ds(t * TILE, TILE), cols] = tile_hits(row, t * TILE, one8, zero8)
        return carry

    lax.fori_loop(0, 8, build, 0)

    top = jnp.maximum(peak(shapes), 1e-30)
    for p, piece in enumerate(f8_pieces(shapes * (256.0 / top))):
        own_lhs[pl.ds(p * rows, rows), :] = piece
    own_unit = top * (1.0 / 256.0)

    def gather_own(a, carry):
        cols = pl.ds(pl.multiple_of(a * elems, elems), elems)
        r = jnp.dot(own_lhs[...], hot[0:nodes, cols], preferred_element_type=F32)
        corners[:, cols] = joined(r, rows, own_unit)
        return carry

    lax.fori_loop(0, 8, gather_own, 0)

    for copy in forward:
        copy.wait()
    has_lo = jnp.where(dom > 0, 1.0, 0.0).astype(F32)
    has_hi = jnp.where(dom < n_dom - 1, 1.0, 0.0).astype(F32)
    outside = jnp.concatenate(
        [halo_dom[0] * has_lo, halo_dom[1] * has_hi, halo_sec[0], halo_sec[1]], axis=1
    )
    top = jnp.maximum(peak(outside), 1e-30)
    for p, piece in enumerate(f8_pieces(outside * (256.0 / top))):
        halo_lhs[pl.ds(p * rows, rows), :] = piece
    halo_unit = top * (1.0 / 256.0)

    def gather_halo(a, carry):
        cols = pl.ds(pl.multiple_of(a * elems, elems), elems)
        r = jnp.dot(halo_lhs[...], hot[nodes : nodes + halo, cols], preferred_element_type=F32)
        corners[:, cols] = corners[:, cols] + joined(r, rows, halo_unit)
        return carry

    lax.fori_loop(0, 8, gather_halo, 0)

    def mode_gradient(e, carry):
        first = pl.multiple_of(e * 128, 128)
        lanes = pl.ds(first, 128)
        for m in range(modes // 16):
            acc = [None] * 9
            for a in range(8):
                for i in range(3):
                    u = corners[
                        pl.ds(i * modes + m * 16, 16),
                        pl.ds(pl.multiple_of(a * elems + first, 128), 128),
                    ]
                    for j in range(3):
                        term = u * grads_ref[j, pl.ds(a, 1), lanes]
                        acc[3 * i + j] = term if acc[3 * i + j] is None else acc[3 * i + j] + term
            for ij in range(9):
                hi, lo = bf_pieces(acc[ij])
                gmode[ij, pl.ds(m * 16, 16), lanes] = hi
                gmode[ij, pl.ds(modes + m * 16, 16), lanes] = hi
                gmode[ij, pl.ds(2 * modes + m * 16, 16), lanes] = lo
        return carry

    lax.fori_loop(0, elems // 128, mode_gradient, 0)

    amp_hi, amp_lo = bf_pieces(amp_ref[...].T)
    amp3 = jnp.concatenate([amp_hi, amp_lo, amp_hi], axis=1)

    def combine(ij, carry):
        piola[ij] = jnp.dot(amp3, gmode[ij], preferred_element_type=F32)
        return carry

    lax.fori_loop(0, 9, combine, 0)

    def stress_rows(r, carry):
        part = pl.ds(pl.multiple_of(r * 8, 8), 8)

        def stress_cols(e, keep):
            lanes = pl.ds(pl.multiple_of(e * 128, 128), 128)
            g = [[piola[3 * i + j, part, lanes] for j in range(3)] for i in range(3)]
            lam, mu = lame_ref[0:1, lanes], lame_ref[1:2, lanes]
            twice = [[None] * 3 for _ in range(3)]
            for i in range(3):
                for j in range(i, 3):
                    quad = g[0][i] * g[0][j] + g[1][i] * g[1][j] + g[2][i] * g[2][j]
                    twice[i][j] = twice[j][i] = g[i][j] + g[j][i] + quad
            trace = (twice[0][0] + twice[1][1] + twice[2][2]) * (0.5 * lam)
            s = [[None] * 3 for _ in range(3)]
            for i in range(3):
                for j in range(i, 3):
                    v = mu * twice[i][j]
                    s[i][j] = s[j][i] = v + trace if i == j else v
            for i in range(3):
                for j in range(3):
                    p = s[i][j] + g[i][0] * s[0][j] + g[i][1] * s[1][j] + g[i][2] * s[2][j]
                    piola[3 * i + j, part, lanes] = p
            return keep

        return lax.fori_loop(0, elems // 128, stress_cols, carry)

    lax.fori_loop(0, combos // 8, stress_rows, 0)

    def project(ij, acc):
        both = jnp.concatenate(bf_pieces(piola[ij]), axis=0)
        return acc + lax.dot_general(
            gmode[ij, pl.ds(modes, 2 * modes), :], both, NT, preferred_element_type=F32
        )

    acc = lax.fori_loop(0, 9, project, jnp.zeros((2 * modes, 2 * combos), F32))
    acc = acc[:modes] + acc[modes:]
    acc = acc[:, :combos] + acc[:, combos:]
    half = modes // 2
    mine[0] = jnp.concatenate([acc[:half], acc[half:]], axis=1)

    def send_stage(s):
        copies = []
        for r, other in enumerate(groups[s]):
            copies.append(
                pltpu.make_async_remote_copy(
                    src_ref=mine.at[s], dst_ref=theirs.at[s, me[s]],
                    send_sem=as_sem.at[s, r], recv_sem=ar_sem.at[s, r],
                    device_id=other, device_id_type=MESH,
                )
            )
            copies[-1].start()
        return copies

    def end_stage(s, copies):
        theirs[s, me[s]] = mine[s]
        for copy in copies:
            copy.wait()
        total = theirs[s, 0]
        for q in range(1, 8):
            total = total + theirs[s, q]
        return total

    stage0 = send_stage(0)

    def corner_forces(e, carry):
        first = pl.multiple_of(e * 128, 128)
        lanes = pl.ds(first, 128)
        for q in range(combos // 32):
            part = pl.ds(q * 32, 32)
            for i in range(3):
                p = [piola[3 * i + j, part, lanes] for j in range(3)]
                for a in range(8):
                    f = (
                        p[0] * grads_ref[0, pl.ds(a, 1), lanes]
                        + p[1] * grads_ref[1, pl.ds(a, 1), lanes]
                        + p[2] * grads_ref[2, pl.ds(a, 1), lanes]
                    )
                    cols = pl.ds(pl.multiple_of(a * elems + first, 128), 128)
                    for t, piece in enumerate(bf_pieces(f)):
                        forces[pl.ds(t * frows + i * combos + q * 32, 32), cols] = piece
        return carry

    lax.fori_loop(0, elems // 128, corner_forces, 0)

    def scatter(first, width):
        def fill(a, carry):
            near = (conn_ref[pl.ds(a, 1), :] - first).astype(jnp.int16)
            slots = lax.broadcasted_iota(jnp.int16, (width, elems), 0)
            cols = pl.ds(pl.multiple_of(a * elems, elems), elems)
            hot_block[0:width, cols] = jnp.where(slots == near, jnp.ones((), BF), jnp.zeros((), BF))
            return carry

        lax.fori_loop(0, 8, fill, 0)
        r = lax.dot_general(forces[...], hot_block[0:width, :], NT, preferred_element_type=F32)
        return r[:frows] + r[frows:]

    backward = []

    def send_back(j, src, dst):
        backward.append(
            pltpu.make_async_remote_copy(
                src_ref=src, dst_ref=dst, send_sem=bs_sem.at[j], recv_sem=br_sem.at[j],
                device_id=halo_to[j], device_id_type=MESH,
            )
        )
        backward[-1].start()

    bk_dom[0] = scatter(nodes, wd)
    send_back(0, bk_dom.at[0], ret_dom.at[1])
    bk_dom[1] = scatter(nodes + wd, wd)
    send_back(1, bk_dom.at[1], ret_dom.at[0])
    both = scatter(nodes + 2 * wd, 2 * ws)
    bk_sec[0] = both[:, :ws]
    bk_sec[1] = both[:, ws:]
    send_back(2, bk_sec.at[0], ret_sec.at[1])
    send_back(3, bk_sec.at[1], ret_sec.at[0])

    mine[1] = end_stage(0, stage0)
    stage1 = send_stage(1)

    def own_block(b, carry):
        first = pl.multiple_of(b * 256, 256)
        out_ref[:, pl.ds(first, 256)] = scatter(first, 256)
        return carry

    blocks = nodes // 256
    lax.fori_loop(0, blocks // 2, own_block, 0)
    mine[2] = end_stage(1, stage1)
    stage2 = send_stage(2)
    lax.fori_loop(blocks // 2, blocks, own_block, 0)
    total = end_stage(2, stage2) * scale
    modal_ref[0:half, :] = total[:, :combos]
    modal_ref[half:modes, :] = total[:, combos:]

    for copy in backward:
        copy.wait()
    returned = jnp.concatenate(
        [ret_dom[0] * has_lo, ret_dom[1] * has_hi, ret_sec[0], ret_sec[1]], axis=1
    )
    r = lax.dot_general(
        jnp.concatenate(bf_pieces(returned), axis=0), hot_send[...], NT, preferred_element_type=F32
    )
    out_ref[...] = out_ref[...] + (r[:frows] + r[frows:])


def local(amplitudes, mode_shapes, shape_grads, lame_params, connectivity, dom_sends, sector_sends):
    modes, _, nodes = mode_shapes.shape
    combos = amplitudes.shape[0]
    elems = connectivity.shape[1]
    wd, ws = dom_sends.shape[1], sector_sends.shape[1]
    rows, frows, halo = 3 * modes, 3 * combos, 2 * wd + 2 * ws
    all_nodes = nodes * lax.axis_size("sector") * lax.axis_size("dom")
    vmem = pl.BlockSpec(memory_space=pltpu.VMEM)
    dma = pltpu.SemaphoreType.DMA
    nodal, modal = pl.pallas_call(
        functools.partial(kernel, 1.0 / math.sqrt(3.0 * all_nodes)),
        out_shape=(
            jax.ShapeDtypeStruct((frows, nodes), F32),
            jax.ShapeDtypeStruct((modes, combos), F32),
        ),
        in_specs=[vmem] * 7,
        out_specs=(vmem, vmem),
        scratch_shapes=[
            pltpu.VMEM((nodes + halo, 8 * elems), F8),
            pltpu.VMEM((nodes, halo), BF),
            pltpu.VMEM((256, 8 * elems), BF),
            pltpu.VMEM((3 * rows, nodes), F8),
            pltpu.VMEM((3 * rows, halo), F8),
            pltpu.VMEM((rows, 8 * elems), F32),
            pltpu.VMEM((9, 3 * modes, elems), BF),
            pltpu.VMEM((9, combos, elems), F32),
            pltpu.VMEM((2 * frows, 8 * elems), BF),
            pltpu.VMEM((2, rows, wd), F32),
            pltpu.VMEM((2, rows, ws), F32),
            pltpu.VMEM((2, rows, wd), F32),
            pltpu.VMEM((2, rows, ws), F32),
            pltpu.VMEM((2, frows, wd), F32),
            pltpu.VMEM((2, frows, ws), F32),
            pltpu.VMEM((2, frows, wd), F32),
            pltpu.VMEM((2, frows, ws), F32),
            pltpu.VMEM((3, modes // 2, 2 * combos), F32),
            pltpu.VMEM((3, 8, modes // 2, 2 * combos), F32),
            dma((4,)), dma((4,)), dma((4,)), dma((4,)), dma((3, 7)), dma((3, 7)),
        ],
        compiler_params=pltpu.CompilerParams(
            collective_id=0, has_side_effects=True, vmem_limit_bytes=56 << 20
        ),
    )(
        amplitudes.T,
        mode_shapes.transpose(1, 0, 2).reshape(rows, nodes),
        shape_grads.transpose(1, 0, 2),
        lame_params,
        connectivity,
        dom_sends,
        sector_sends,
    )
    return nodal.reshape(3, combos, nodes).transpose(1, 0, 2), modal.T


def solution(mesh):
    placed = (
        P(),
        P(None, None, ("sector", "dom")),
        P(None, None, ("sector", "dom")),
        P(None, ("sector", "dom")),
        P(None, ("sector", "dom")),
        P(None, ("sector", "dom")),
        P(None, ("sector", "dom")),
    )
    return jax.shard_map(
        local,
        mesh=mesh,
        in_specs=placed,
        out_specs=(P(None, None, ("sector", "dom")), P()),
        check_vma=False,
    )
```

time: 309 us -> 67.6 us (0.22)
  blocking collectives: 111 us -> 0 us
  local copies, waits for them, and re-layouts: 87.5 us -> 2.71 us
  other arithmetic: 66.7 us -> 0 us
  Pallas kernels: 0 us -> 63.2 us
  starting transfers between devices: 24.6 us -> 0 us
  waiting for transfers between devices: 14.3 us -> 0 us
    psum x1 -> x0, blocking collectives: 111 us -> none  [local(): modal_total = lax.psum(partial_modal, ('sector', 'dom'))]
    pallas_call x0 -> x1, Pallas kernels: none -> 63.2 us  [local(): pl.pallas_call(functools.partial(kernel, 1.0 / math.sqrt(3.0 * all_nodes)...]
    scatter-add x6 -> x0, other arithmetic: 57.4 us -> none  [the longest x4 50.6 us: element_forces(): accum.at[:, slot_index]]
    gather x10 -> x0, local copies, waits for them, and re-layouts: 50.3 us -> none  [the longest x8 47.8 us: element_forces(): jnp.take(extended, slot_index, axis=1, mode='fill', fill_value=0.0)]
    ppermute x8 -> x0, starting transfers between devices: 24.6 us -> none  [the longest x4 15 us: padded(): lax.ppermute(tail, axis, [(i, (i + 1) % count) for i in range(ends)])]
    ppermute x8 -> x0, waiting for transfers between devices: 14.3 us -> none  [the longest x4 13.4 us: padded(): lax.ppermute(head, axis, [((i + 1) % count, i) for i in range(ends)])]
    slice x17 -> x0, local copies, waits for them, and re-layouts: 13.7 us -> none  [the longest x4 5.3 us: element_forces(): gradients[corner][None, None, :, :]]
    reshape x9 -> x0, local copies, waits for them, and re-layouts: 9.63 us -> none  [the longest x4 7.39 us: element_forces(): corner_forces.reshape(3 * combo_total, 8 * elem_total)]
  transfers between devices with their start and end apart: 8 -> 0, of which waited for: 3 -> 0; matrix products, arithmetic and copies ran while one was open for 2% -> 0% of each run, Pallas kernels for 0% -> 0%
where the time goes in v1:
time: 67.6 us; the launch traced here: 66.5 us
  Pallas kernels  63.2 us (93%)
  local copies, waits for them, and re-layouts  2.71 us (4%)
    pallas_call x1, Pallas kernels, local(): pl.pallas_call(functools.partial(kernel, 1.0 / math.sqrt(3.0 * all_nodes)...  63.2 us
    unnamed x4, local copies, waits for them, and re-layouts  2.71 us

profile of v1, /device:TPU:1, one launch (start us, length us, event | category | flops | bytes accessed | tf_op | source)
XLA Modules:
  0.0 66.5 jit_solution(14894565908161549474)
XLA Ops:
  0.6 63.2 %shard_map.86 = (f32[192,1024]{1,0:T(8,128)}, f32[48,64]{1,0:T(8,128)}) custom-call(f32[48,64]{1,0:T(8,128)} %bitcast.12, f32[144,1024]{1,0:T(8,128)} %bitcast.10, f32[3,8,1024]{2,1,0:T(8,128)} %bitcast.11, f32[2,1024]{1,0:T(2,128)} %lame_ref.1, s32[8,1024]{1,0:T(8,128)} %conn_ref.1, s32[2,256]{1,0:T(2,128)} %dsend_ref.1, s32[2,128]{1,0:T(2,128)} %ssend_ref.1), custom_call_target="tpu_custom_call" | custom-call | tf_op jit(solution)/shard_map/pallas_call | solution.py:354
  63.8 0.0 copy-start
  63.8 2.1 %copy.11 = f32[64,3,1024]{2,0,1:T(8,128)} copy(f32[64,3,1024]{2,0,1:T(8,128)} %bitcast.9) | data formatting | bytes 1572864
  65.9 0.0 copy-done
  65.9 0.6 copy.12
Async XLA Ops:
  63.8 2.1 %copy-start = (f32[48,64]{1,0:T(8,128)S(1)}, f32[48,64]{1,0:T(8,128)}, u32[]{:S(2)}) copy-start(f32[48,64]{1,0:T(8,128)} %get-tuple-element.5) | copy-start | bytes 36868

commit v2 on v1

--- a/solution.py
+++ b/solution.py
@@ -45,25 +45,26 @@
 
 
 def stage_index(stage, y, x, c, z):
-    return (x * 2 + c, y * 2 + z % 2, z // 2)[stage]
+    return (z // 2, y * 2 + z % 2, x * 2 + c)[stage]
 
 
 def stage_device(stage, i, y, x, c, z):
     if stage == 0:
-        x, c = i // 2, i % 2
+        z = i * 2 + z % 2
     elif stage == 1:
         y, z = i // 2, (z // 2) * 2 + i % 2
     else:
-        z = i * 2 + z % 2
+        x, c = i // 2, i % 2
     return (y * 4 + (x % 2) * 2 + c, z * 2 + x // 2)
 
 
 def kernel(
-    scale, amp_ref, modes_ref, grads_ref, lame_ref, conn_ref, dsend_ref, ssend_ref,
+    scale, amp_hbm, modes_hbm, grads_hbm, lame_hbm, conn_hbm, dsend_hbm, ssend_hbm,
     out_ref, modal_ref,
+    amp_ref, modes_ref, grads_ref, lame_ref, conn_ref, dsend_ref, ssend_ref,
     hot, hot_send, hot_block, own_lhs, halo_lhs, corners, gmode, piola, forces,
     pk_dom, pk_sec, halo_dom, halo_sec, bk_dom, bk_sec, ret_dom, ret_sec, mine, theirs,
-    fs_sem, fr_sem, bs_sem, br_sem, as_sem, ar_sem,
+    in_sem, fs_sem, fr_sem, bs_sem, br_sem, as_sem, ar_sem,
 ):
     n_sec, n_dom = lax.axis_size("sector"), lax.axis_size("dom")
     sec, dom = lax.axis_index("sector"), lax.axis_index("dom")
@@ -83,17 +84,36 @@
         [stage_device(s, lax.rem(me[s] + r, 8), y, x, c, z) for r in range(1, 8)] for s in range(3)
     ]
 
+    loads = [
+        pltpu.make_async_copy(src, dst, in_sem.at[j])
+        for j, (src, dst) in enumerate(
+            (
+                (dsend_hbm, dsend_ref),
+                (ssend_hbm, ssend_ref),
+                (modes_hbm, modes_ref),
+                (conn_hbm, conn_ref),
+                (grads_hbm, grads_ref),
+                (amp_hbm, amp_ref),
+                (lame_hbm, lame_ref),
+            )
+        )
+    ]
+    for load in loads:
+        load.start()
     barrier = pltpu.get_barrier_semaphore()
     everyone = halo_to + groups[0] + groups[1] + groups[2]
     for other in everyone:
         pl.semaphore_signal(barrier, inc=1, device_id=other, device_id_type=MESH)
 
+    loads[0].wait()
+    loads[1].wait()
     for first, width, send in ((0, wd, dsend_ref), (2 * wd, ws, ssend_ref)):
         for row in range(2):
             cols = pl.ds(first + row * width, width)
             slots = lax.broadcasted_iota(jnp.int32, (nodes, width), 0)
             hot_send[:, cols] = jnp.where(slots == send[row : row + 1, :], 1.0, 0.0).astype(BF)
 
+    loads[2].wait()
     shapes = modes_ref[...]
     packets = jnp.dot(
         jnp.concatenate(bf_pieces(shapes), axis=0), hot_send[...], preferred_element_type=F32
@@ -121,29 +141,26 @@
         )
         forward[-1].start()
 
+    for load in loads[3:]:
+        load.wait()
     one8, zero8 = jnp.ones((TILE, elems), F8), jnp.zeros((TILE, elems), F8)
 
-    def build(a, carry):
-        row = conn_ref[pl.ds(a, 1), :]
-        cols = pl.ds(pl.multiple_of(a * elems, elems), elems)
-        for t in range((nodes + halo) // TILE):
-            hot[pl.ds(t * TILE, TILE), cols] = tile_hits(row, t * TILE, one8, zero8)
-        return carry
-
-    lax.fori_loop(0, 8, build, 0)
+    def gather(lhs, first, count, a, unit):
+        room = hot.at[a % 2]
+        for t in range(count // TILE):
+            room[pl.ds(t * TILE, TILE), :] = tile_hits(
+                conn_ref[pl.ds(a, 1), :], first + t * TILE, one8, zero8
+            )
+        r = jnp.dot(lhs[...], room[0:count, :], preferred_element_type=F32)
+        return joined(r, rows, unit)
 
     top = jnp.maximum(peak(shapes), 1e-30)
     for p, piece in enumerate(f8_pieces(shapes * (256.0 / top))):
         own_lhs[pl.ds(p * rows, rows), :] = piece
     own_unit = top * (1.0 / 256.0)
 
-    def gather_own(a, carry):
-        cols = pl.ds(pl.multiple_of(a * elems, elems), elems)
-        r = jnp.dot(own_lhs[...], hot[0:nodes, cols], preferred_element_type=F32)
-        corners[:, cols] = joined(r, rows, own_unit)
-        return carry
-
-    lax.fori_loop(0, 8, gather_own, 0)
+    for a in range(8):
+        corners[:, pl.ds(a * elems, elems)] = gather(own_lhs, 0, nodes, a, own_unit)
 
     for copy in forward:
         copy.wait()
@@ -157,13 +174,9 @@
         halo_lhs[pl.ds(p * rows, rows), :] = piece
     halo_unit = top * (1.0 / 256.0)
 
-    def gather_halo(a, carry):
-        cols = pl.ds(pl.multiple_of(a * elems, elems), elems)
-        r = jnp.dot(halo_lhs[...], hot[nodes : nodes + halo, cols], preferred_element_type=F32)
-        corners[:, cols] = corners[:, cols] + joined(r, rows, halo_unit)
-        return carry
-
-    lax.fori_loop(0, 8, gather_halo, 0)
+    for a in range(8):
+        cols = pl.ds(a * elems, elems)
+        corners[:, cols] = corners[:, cols] + gather(halo_lhs, nodes, halo, a, halo_unit)
 
     def mode_gradient(e, carry):
         first = pl.multiple_of(e * 128, 128)
@@ -181,9 +194,10 @@
                         acc[3 * i + j] = term if acc[3 * i + j] is None else acc[3 * i + j] + term
             for ij in range(9):
                 hi, lo = bf_pieces(acc[ij])
-                gmode[ij, pl.ds(m * 16, 16), lanes] = hi
-                gmode[ij, pl.ds(modes + m * 16, 16), lanes] = hi
-                gmode[ij, pl.ds(2 * modes + m * 16, 16), lanes] = lo
+                cols = pl.ds(pl.multiple_of(ij * elems + first, 128), 128)
+                gmode[pl.ds(m * 16, 16), cols] = hi
+                gmode[pl.ds(modes + m * 16, 16), cols] = hi
+                gmode[pl.ds(2 * modes + m * 16, 16), cols] = lo
         return carry
 
     lax.fori_loop(0, elems // 128, mode_gradient, 0)
@@ -191,18 +205,16 @@
     amp_hi, amp_lo = bf_pieces(amp_ref[...].T)
     amp3 = jnp.concatenate([amp_hi, amp_lo, amp_hi], axis=1)
 
-    def combine(ij, carry):
-        piola[ij] = jnp.dot(amp3, gmode[ij], preferred_element_type=F32)
-        return carry
-
-    lax.fori_loop(0, 9, combine, 0)
+    piola[...] = jnp.dot(amp3, gmode[...], preferred_element_type=F32)
 
     def stress_rows(r, carry):
         part = pl.ds(pl.multiple_of(r * 8, 8), 8)
 
         def stress_cols(e, keep):
-            lanes = pl.ds(pl.multiple_of(e * 128, 128), 128)
-            g = [[piola[3 * i + j, part, lanes] for j in range(3)] for i in range(3)]
+            first = pl.multiple_of(e * 128, 128)
+            lanes = pl.ds(first, 128)
+            at = [pl.ds(pl.multiple_of(ij * elems + first, 128), 128) for ij in range(9)]
+            g = [[piola[part, at[3 * i + j]] for j in range(3)] for i in range(3)]
             lam, mu = lame_ref[0:1, lanes], lame_ref[1:2, lanes]
             twice = [[None] * 3 for _ in range(3)]
             for i in range(3):
@@ -218,20 +230,17 @@
             for i in range(3):
                 for j in range(3):
                     p = s[i][j] + g[i][0] * s[0][j] + g[i][1] * s[1][j] + g[i][2] * s[2][j]
-                    piola[3 * i + j, part, lanes] = p
+                    piola[part, at[3 * i + j]] = p
             return keep
 
         return lax.fori_loop(0, elems // 128, stress_cols, carry)
 
     lax.fori_loop(0, combos // 8, stress_rows, 0)
 
-    def project(ij, acc):
-        both = jnp.concatenate(bf_pieces(piola[ij]), axis=0)
-        return acc + lax.dot_general(
-            gmode[ij, pl.ds(modes, 2 * modes), :], both, NT, preferred_element_type=F32
-        )
-
-    acc = lax.fori_loop(0, 9, project, jnp.zeros((2 * modes, 2 * combos), F32))
+    both = jnp.concatenate(bf_pieces(piola[...]), axis=0)
+    acc = lax.dot_general(
+        gmode[modes : 3 * modes, :], both, NT, preferred_element_type=F32
+    )
     acc = acc[:modes] + acc[modes:]
     acc = acc[:, :combos] + acc[:, combos:]
     half = modes // 2
@@ -267,7 +276,10 @@
         for q in range(combos // 32):
             part = pl.ds(q * 32, 32)
             for i in range(3):
-                p = [piola[3 * i + j, part, lanes] for j in range(3)]
+                p = [
+                    piola[part, pl.ds(pl.multiple_of((3 * i + j) * elems + first, 128), 128)]
+                    for j in range(3)
+                ]
                 for a in range(8):
                     f = (
                         p[0] * grads_ref[0, pl.ds(a, 1), lanes]
@@ -282,14 +294,11 @@
     lax.fori_loop(0, elems // 128, corner_forces, 0)
 
     def scatter(first, width):
-        def fill(a, carry):
-            near = (conn_ref[pl.ds(a, 1), :] - first).astype(jnp.int16)
+        for a in range(8):
+            near = (conn_ref[a : a + 1, :] - first).astype(jnp.int16)
             slots = lax.broadcasted_iota(jnp.int16, (width, elems), 0)
-            cols = pl.ds(pl.multiple_of(a * elems, elems), elems)
+            cols = pl.ds(a * elems, elems)
             hot_block[0:width, cols] = jnp.where(slots == near, jnp.ones((), BF), jnp.zeros((), BF))
-            return carry
-
-        lax.fori_loop(0, 8, fill, 0)
         r = lax.dot_general(forces[...], hot_block[0:width, :], NT, preferred_element_type=F32)
         return r[:frows] + r[frows:]
 
@@ -305,17 +314,18 @@
         backward[-1].start()
 
     bk_dom[0] = scatter(nodes, wd)
-    send_back(0, bk_dom.at[0], ret_dom.at[1])
+    mine[1] = end_stage(0, stage0)
+    stage1 = send_stage(1)
     bk_dom[1] = scatter(nodes + wd, wd)
-    send_back(1, bk_dom.at[1], ret_dom.at[0])
     both = scatter(nodes + 2 * wd, 2 * ws)
     bk_sec[0] = both[:, :ws]
     bk_sec[1] = both[:, ws:]
+    mine[2] = end_stage(1, stage1)
+    stage2 = send_stage(2)
+    send_back(0, bk_dom.at[0], ret_dom.at[1])
+    send_back(1, bk_dom.at[1], ret_dom.at[0])
     send_back(2, bk_sec.at[0], ret_sec.at[1])
     send_back(3, bk_sec.at[1], ret_sec.at[0])
-
-    mine[1] = end_stage(0, stage0)
-    stage1 = send_stage(1)
 
     def own_block(b, carry):
         first = pl.multiple_of(b * 256, 256)
@@ -323,10 +333,7 @@
         return carry
 
     blocks = nodes // 256
-    lax.fori_loop(0, blocks // 2, own_block, 0)
-    mine[2] = end_stage(1, stage1)
-    stage2 = send_stage(2)
-    lax.fori_loop(blocks // 2, blocks, own_block, 0)
+    lax.fori_loop(0, blocks, own_block, 0)
     total = end_stage(2, stage2) * scale
     modal_ref[0:half, :] = total[:, :combos]
     modal_ref[half:modes, :] = total[:, combos:]
@@ -357,17 +364,24 @@
             jax.ShapeDtypeStruct((frows, nodes), F32),
             jax.ShapeDtypeStruct((modes, combos), F32),
         ),
-        in_specs=[vmem] * 7,
+        in_specs=[pl.BlockSpec(memory_space=pltpu.HBM)] * 7,
         out_specs=(vmem, vmem),
         scratch_shapes=[
-            pltpu.VMEM((nodes + halo, 8 * elems), F8),
+            pltpu.VMEM((modes, combos), F32),
+            pltpu.VMEM((rows, nodes), F32),
+            pltpu.VMEM((3, 8, elems), F32),
+            pltpu.VMEM((2, elems), F32),
+            pltpu.VMEM((8, elems), jnp.int32),
+            pltpu.VMEM((2, wd), jnp.int32),
+            pltpu.VMEM((2, ws), jnp.int32),
+            pltpu.VMEM((2, nodes, elems), F8),
             pltpu.VMEM((nodes, halo), BF),
             pltpu.VMEM((256, 8 * elems), BF),
             pltpu.VMEM((3 * rows, nodes), F8),
             pltpu.VMEM((3 * rows, halo), F8),
             pltpu.VMEM((rows, 8 * elems), F32),
-            pltpu.VMEM((9, 3 * modes, elems), BF),
-            pltpu.VMEM((9, combos, elems), F32),
+            pltpu.VMEM((3 * modes, 9 * elems), BF),
+            pltpu.VMEM((combos, 9 * elems), F32),
             pltpu.VMEM((2 * frows, 8 * elems), BF),
             pltpu.VMEM((2, rows, wd), F32),
             pltpu.VMEM((2, rows, ws), F32),
@@ -379,7 +393,7 @@
             pltpu.VMEM((2, frows, ws), F32),
             pltpu.VMEM((3, modes // 2, 2 * combos), F32),
             pltpu.VMEM((3, 8, modes // 2, 2 * combos), F32),
-            dma((4,)), dma((4,)), dma((4,)), dma((4,)), dma((3, 7)), dma((3, 7)),
+            dma((7,)), dma((4,)), dma((4,)), dma((4,)), dma((4,)), dma((3, 7)), dma((3, 7)),
         ],
         compiler_params=pltpu.CompilerParams(
             collective_id=0, has_side_effects=True, vmem_limit_bytes=56 << 20

time: 67.6 us -> 66.5 us (0.984); the launches traced: 66.5 us -> 66.3 us
  no operation moved by 1% of the time
where the time goes in v2:
time: 66.5 us; the launch traced here: 66.3 us
  Pallas kernels  63 us (95%)
  local copies, waits for them, and re-layouts  2.71 us (4%)
    pallas_call x1, Pallas kernels, local(): pl.pallas_call(functools.partial(kernel, 1.0 / math.sqrt(3.0 * all_nodes)...  63 us
    unnamed x4, local copies, waits for them, and re-layouts  2.71 us

profile of v2, /device:TPU:1, one launch (start us, length us, event | category | flops | bytes accessed | tf_op | source)
XLA Modules:
  0.0 66.3 jit_solution(17109903200969919999)
XLA Ops:
  0.6 63.0 %shard_map.86 = (f32[192,1024]{1,0:T(8,128)}, f32[48,64]{1,0:T(8,128)}) custom-call(f32[48,64]{1,0:T(8,128)} %bitcast.12, f32[144,1024]{1,0:T(8,128)} %bitcast.10, f32[3,8,1024]{2,1,0:T(8,128)} %bitcast.11, f32[2,1024]{1,0:T(2,128)} %lame_hbm.1, s32[8,1024]{1,0:T(8,128)} %conn_hbm.1, s32[2,256]{1,0:T(2,128)} %dsend_hbm.1, s32[2,128]{1,0:T(2,128)} %ssend_hbm.1), custom_call_target="tpu_custom_call" | custom-call | tf_op jit(solution)/shard_map/pallas_call | solution.py:361
  63.6 0.0 copy-start
  63.6 2.1 %copy.11 = f32[64,3,1024]{2,0,1:T(8,128)} copy(f32[64,3,1024]{2,0,1:T(8,128)} %bitcast.9) | data formatting | bytes 1572864
  65.7 0.0 copy-done
  65.7 0.6 copy.12
Async XLA Ops:
  63.6 2.1 %copy-start = (f32[48,64]{1,0:T(8,128)S(1)}, f32[48,64]{1,0:T(8,128)}, u32[]{:S(2)}) copy-start(f32[48,64]{1,0:T(8,128)} %get-tuple-element.5) | copy-start | bytes 36868

commit v3 on v2

--- a/solution.py
+++ b/solution.py
@@ -314,16 +314,14 @@
         backward[-1].start()
 
     bk_dom[0] = scatter(nodes, wd)
+    send_back(0, bk_dom.at[0], ret_dom.at[1])
+    bk_dom[1] = scatter(nodes + wd, wd)
+    send_back(1, bk_dom.at[1], ret_dom.at[0])
     mine[1] = end_stage(0, stage0)
     stage1 = send_stage(1)
-    bk_dom[1] = scatter(nodes + wd, wd)
     both = scatter(nodes + 2 * wd, 2 * ws)
     bk_sec[0] = both[:, :ws]
     bk_sec[1] = both[:, ws:]
-    mine[2] = end_stage(1, stage1)
-    stage2 = send_stage(2)
-    send_back(0, bk_dom.at[0], ret_dom.at[1])
-    send_back(1, bk_dom.at[1], ret_dom.at[0])
     send_back(2, bk_sec.at[0], ret_sec.at[1])
     send_back(3, bk_sec.at[1], ret_sec.at[0])
 
@@ -333,7 +331,10 @@
         return carry
 
     blocks = nodes // 256
-    lax.fori_loop(0, blocks, own_block, 0)
+    lax.fori_loop(0, blocks // 2, own_block, 0)
+    mine[2] = end_stage(1, stage1)
+    stage2 = send_stage(2)
+    lax.fori_loop(blocks // 2, blocks, own_block, 0)
     total = end_stage(2, stage2) * scale
     modal_ref[0:half, :] = total[:, :combos]
     modal_ref[half:modes, :] = total[:, combos:]
@@ -396,16 +397,21 @@
             dma((7,)), dma((4,)), dma((4,)), dma((4,)), dma((4,)), dma((3, 7)), dma((3, 7)),
         ],
         compiler_params=pltpu.CompilerParams(
-            collective_id=0, has_side_effects=True, vmem_limit_bytes=56 << 20
+            collective_id=0, has_side_effects=True, vmem_limit_bytes=36 << 20
         ),
     )(
-        amplitudes.T,
-        mode_shapes.transpose(1, 0, 2).reshape(rows, nodes),
-        shape_grads.transpose(1, 0, 2),
-        lame_params,
-        connectivity,
-        dom_sends,
-        sector_sends,
+        *(
+            pltpu.with_memory_space_constraint(x, pltpu.HBM)
+            for x in (
+                amplitudes.T,
+                mode_shapes.transpose(1, 0, 2).reshape(rows, nodes),
+                shape_grads.transpose(1, 0, 2),
+                lame_params,
+                connectivity,
+                dom_sends,
+                sector_sends,
+            )
+        )
     )
     return nodal.reshape(3, combos, nodes).transpose(1, 0, 2), modal.T
 

time: 66.5 us -> 62.2 us (0.935)
  Pallas kernels: 63 us -> 59.9 us
  local copies, waits for them, and re-layouts: 2.71 us -> 1.49 us
    pallas_call x1, Pallas kernels: 63 us -> 59.9 us  [local(): pl.pallas_call(functools.partial(kernel, 1.0 / math.sqrt(3.0 * all_nodes)...]
    unnamed x4 -> x2, local copies, waits for them, and re-layouts: 2.71 us -> 1.49 us
where the time goes in v3:
time: 62.2 us; the launch traced here: 62.1 us
  Pallas kernels  59.9 us (96%)
  local copies, waits for them, and re-layouts  1.49 us (2%)
  between operations  0.64 us (1%)
    pallas_call x1, Pallas kernels, local(): pl.pallas_call(functools.partial(kernel, 1.0 / math.sqrt(3.0 * all_nodes)...  59.9 us
    unnamed x2, local copies, waits for them, and re-layouts  1.49 us

profile of v3, /device:TPU:1, one launch (start us, length us, event | category | flops | bytes accessed | tf_op | source)
XLA Modules:
  0.0 62.1 jit_solution(3387870326012930432)
XLA Ops:
  0.6 59.9 %shard_map.86 = (f32[192,1024]{1,0:T(8,128)S(1)}, f32[48,64]{1,0:T(8,128)S(1)}) custom-call(f32[48,64]{1,0:T(8,128)} %bitcast.13, f32[144,1024]{1,0:T(8,128)} %bitcast.11, f32[3,8,1024]{2,1,0:T(8,128)} %bitcast.12, f32[2,1024]{1,0:T(2,128)} %lame_hbm.1, s32[8,1024]{1,0:T(8,128)} %conn_hbm.1, s32[2,256]{1,0:T(2,128)} %dsend_hbm.1, s32[2,128]{1,0:T(2,128)} %ssend_hbm.1), custom_call_target="tpu_custom_call" | custom-call | tf_op jit(solution)/shard_map/pallas_call | solution.py:362
  60.6 0.9 %copy.11 = f32[64,3,1024]{2,0,1:T(8,128)} copy(f32[64,3,1024]{2,0,1:T(8,128)S(1)} %bitcast.9) | data formatting | bytes 1572864
  61.5 0.6 copy.12
